TPU v7x, 32 devices: a whole 2x2x4 slice. The times are simulated.
32 devices in a mesh: dp: 8 (over z, core), mp: 4 (over y, x).
Axes of the slice: x: 2, y: 2, z: 4, core: 2. Of those that a mesh axis runs over, the one named last changes fastest.
Arguments:
- student_in: bfloat16 [128, 6144], P(None, 'mp'), may hold values from -6 to 6
- teacher_hidden: bfloat16 [8192, 128], P('dp'), may hold values from -6 to 6
- w_up: bfloat16 [24576, 6144], P('dp', 'mp'), may hold values from -0.078125 to 0.078125
- w_down: bfloat16 [24576, 6144], P('dp', 'mp'), may hold values from -0.0390625 to 0.0390625
- w_proj: bfloat16 [8192, 6144], P('dp', 'mp'), may hold values from -0.0625 to 0.0625
Outputs:
- grad_up: float32 [24576, 6144], P('dp', 'mp')
- grad_down: float32 [24576, 6144], P('dp', 'mp')
- grad_proj: float32 [8192, 6144], P('dp', 'mp')
All inputs are finite; a program needn't handle non-finite values.
Results may differ from a plain program's by a relative error of at most 0.005.
Values may be sent and summed in bfloat16 or wider, within the bound.
No kernel may reach another device: no remote copies, remote signals or barrier semaphores. Data moves between devices by JAX's collectives and lax.ppermute only.
A program may use at most 128 MiB of HBM per device.

v0:
```python
import math

import jax
import jax.numpy as jnp
from jax import lax
from jax.sharding import PartitionSpec as P


def contract_first(left, right):
    return lax.dot_general(
        left, right, (((0,), (0,)), ((), ())), preferred_element_type=jnp.float32
    )


def contract_last(left, right):
    return lax.dot_general(
        left, right, (((1,), (1,)), ((), ())), preferred_element_type=jnp.float32
    )


def body(student_in, teacher_hidden, w_up, w_down, w_proj):
    tokens_all = student_in.shape[0]
    partial_pre = contract_last(w_up, student_in)
    pre = lax.psum(partial_pre, "mp")
    active = jnp.maximum(pre, 0.0)
    hidden = (active * active).astype(jnp.bfloat16)
    student_part = contract_first(hidden, w_down)
    target_part = contract_first(teacher_hidden, w_proj)
    residual = lax.psum_scatter(student_part - target_part, "dp", scatter_dimension=0, tiled=True)
    d_local = (residual * (1.0 / math.sqrt(tokens_all))).astype(jnp.bfloat16)
    piece = lax.all_gather(d_local, "dp", axis=0, tiled=True)
    proj_acc = jnp.zeros(w_proj.shape, jnp.float32)
    down_acc = jnp.dot(hidden, piece, preferred_element_type=jnp.float32)
    proj_acc = proj_acc - jnp.dot(teacher_hidden, piece, preferred_element_type=jnp.float32)
    grad_cols = contract_last(w_down, piece)
    d_hidden = lax.psum(grad_cols, "mp")
    d_pre = (d_hidden * (2.0 * active)).astype(jnp.bfloat16)
    grad_up = jnp.dot(d_pre, student_in, preferred_element_type=jnp.float32)
    return (grad_up, down_acc, proj_acc)


def solution(mesh):
    return jax.shard_map(
        body,
        mesh=mesh,
        in_specs=(P(None, "mp"), P("dp", None), P("dp", "mp"), P("dp", "mp"), P("dp", "mp")),
        out_specs=(P("dp", "mp"), P("dp", "mp"), P("dp", "mp")),
        check_vma=False,
    )
```

profile of v0, /device:TPU:0, one launch (start us, length us, event | category | flops | bytes accessed | tf_op | source)
XLA Modules:
  0.0 216.5 jit_solution(6784596743819639396)
XLA Ops:
  7.2 0.0 copy-start
  7.2 0.0 all-reduce.3.cloned.1.call-start
  7.2 7.6 %fusion.9 = f32[3072,128]{1,0:T(8,128)} fusion(bf16[3072,1536]{1,0:T(8,128)(2,1)} %param.7, bf16[128,1536]{1,0:T(8,128)(2,1)} %param.5), kind=kOutput, calls=%fused_computation.15 | convolution fusion | flops 1207959552 | bytes 11403264 | tf_op jit(solution)/shard_map/dot_general | solution.py:16
  14.8 0.0 all-reduce.3.cloned.1.call-update
  14.8 0.0 copy-start.4
  14.8 0.0 reduce-scatter.2.cloned.1.call-start
  14.9 63.5 %all-reduce.3.cloned.1.call-done = f32[3072,128]{1,0:T(8,128)} async-done(((f32[3072,128]{1,0:T(8,128)}), f32[3072,128]{1,0:T(8,128)}) %all-reduce.3.cloned.1.call-update) | async-done | bytes 1572880 | tf_op jit(solution)/shard_map/psum | solution.py:24
  78.4 5.6 %fusion.4 = f32[128,1536]{1,0:T(8,128)S(1)} fusion(bf16[3072,1536]{1,0:T(8,128)(2,1)} %param.8, f32[3072,128]{1,0:T(8,128)} %all-reduce.3.cloned.1.call-done), kind=kOutput, calls=%fused_computation.9 | convolution fusion | flops 1209139200 | bytes 11796480 | tf_op jit(solution)/shard_map/dot_general | solution.py:10
  84.1 0.0 copy-done
  84.1 0.0 copy-done.4
  84.1 1.5 convolution_subtract_fusion
  85.6 0.0 reduce-scatter.2.cloned.1.call-update
  85.6 0.0 all-reduce.5.cloned.1.call-start
  85.6 31.9 %reduce-scatter.2.cloned.1.call-done = f32[16,1536]{1,0:T(8,128)} async-done(((f32[128,1536]{1,0:T(8,128)}), f32[16,1536]{1,0:T(8,128)}) %reduce-scatter.2.cloned.1.call-update) | async-done | bytes 98320 | tf_op jit(solution)/shard_map/reduce_scatter | solution.py:29
  117.6 0.9 multiply_convert_fusion.5
  118.5 14.5 %all_gather.3 = bf16[128,1536]{1,0:T(8,128)(2,1)S(1)} all-gather(bf16[16,1536]{1,0:T(8,128)(2,1)S(1)} %multiply_convert_fusion.5), channel_id=1, replica_groups=mesh['dp'=8,'mp'=4] {'dp'}, dimensions={0}, use_global_device_ids=true | all-gather | bytes 442368 | tf_op jit(solution)/shard_map/all_gather | solution.py:31
  132.9 7.4 %convolution_bitcast_fusion = f32[3072,128]{1,0:T(8,128)} fusion(bf16[128,1536]{1,0:T(8,128)(2,1)S(1)} %all_gather.3, bf16[3072,1536]{1,0:T(8,128)(2,1)} %param.8), kind=kOutput, calls=%fused_computation.1 | convolution fusion | flops 1207959552 | bytes 11403264 | tf_op jit(solution)/shard_map/dot_general | solution.py:16
  140.4 0.0 all-reduce.5.cloned.1.call-update
  140.4 3.7 %subtract_bitcast_fusion = f32[1024,1536]{0,1:T(8,128)} fusion(bf16[128,1536]{1,0:T(8,128)(2,1)S(1)} %all_gather.3, bf16[1024,128]{1,0:T(8,128)(2,1)S(1)} %copy-done.4), kind=kOutput, calls=%fused_computation | convolution fusion | flops 404226048 | bytes 6946816 | tf_op jit(solution)/shard_map/dot_general | solution.py:34
  144.1 0.0 copy-start.2
  144.1 6.7 %copy.8 = f32[1024,1536]{1,0:T(8,128)} copy(f32[1024,1536]{0,1:T(8,128)} %subtract_bitcast_fusion) | data formatting | bytes 12582912
  150.9 0.0 copy-done.2
  150.9 0.0 copy-start.3
  150.9 8.2 %fusion.3 = f32[3072,1536]{1,0:T(8,128)} fusion(bf16[128,1536]{1,0:T(8,128)(2,1)S(1)} %all_gather.3, f32[3072,128]{1,0:T(8,128)S(1)} %copy-done.2), kind=kOutput, calls=%fused_computation.8 | convolution fusion | flops 1209139200 | bytes 20840448 | tf_op jit(solution)/shard_map/dot_general | solution.py:33
  159.1 40.6 %all-reduce.5.cloned.1.call-done = f32[3072,128]{1,0:T(8,128)} async-done(((f32[3072,128]{1,0:T(8,128)}), f32[3072,128]{1,0:T(8,128)}) %all-reduce.5.cloned.1.call-update) | async-done | bytes 1572880 | tf_op jit(solution)/shard_map/psum | solution.py:36
  199.7 0.0 copy-done.3
  199.7 0.0 copy-start.1
  199.7 10.3 %fusion = f32[3072,1536]{1,0:T(8,128)} fusion(bf16[128,1536]{1,0:T(8,128)(2,1)S(1)} %copy-done.3, f32[3072,128]{1,0:T(8,128)} %all-reduce.5.cloned.1.call-done, f32[3072,128]{1,0:T(8,128)} %all-reduce.3.cloned.1.call-done), kind=kOutput, calls=%fused_computation.5 | convolution fusion | flops 1209532416 | bytes 22413312 | tf_op jit(solution)/shard_map/dot_general | solution.py:38
  210.0 0.0 copy-done.1
Async XLA Ops:
  7.2 76.9 %copy-start = (bf16[1024,1536]{1,0:T(8,128)(2,1)S(1)}, bf16[1024,1536]{1,0:T(8,128)(2,1)}, u32[]{:S(2)}) copy-start(bf16[1024,1536]{1,0:T(8,128)(2,1)} %param.9) | copy-start | bytes 9437188
  7.2 71.3 %all-reduce.3.cloned.1.call-start = ((), (), s32[]{:S(2)}) async-start(), calls=%async_computation.1 | async-start | bytes 3145728 | tf_op jit(solution)/shard_map/psum | solution.py:24
  14.8 69.2 %copy-start.4 = (bf16[1024,128]{1,0:T(8,128)(2,1)S(1)}, bf16[1024,128]{1,0:T(8,128)(2,1)}, u32[]{:S(2)}) copy-start(bf16[1024,128]{1,0:T(8,128)(2,1)} %param.6) | copy-start | bytes 786436
  14.8 102.7 %reduce-scatter.2.cloned.1.call-start = ((), (), s32[]{:S(2)}) async-start(), calls=%async_computation.2 | async-start | bytes 884736 | tf_op jit(solution)/shard_map/reduce_scatter | solution.py:29
  85.6 114.1 %all-reduce.5.cloned.1.call-start = ((), (), s32[]{:S(2)}) async-start(), calls=%async_computation.3 | async-start | bytes 3145728 | tf_op jit(solution)/shard_map/psum | solution.py:36
  144.1 6.7 %copy-start.2 = (f32[3072,128]{1,0:T(8,128)S(1)}, f32[3072,128]{1,0:T(8,128)}, u32[]{:S(2)}) copy-start(f32[3072,128]{1,0:T(8,128)} %all-reduce.3.cloned.1.call-done) | copy-start | bytes 4718596
  150.9 48.8 %copy-start.3 = (bf16[128,1536]{1,0:T(8,128)(2,1)S(1)}, bf16[128,1536]{1,0:T(8,128)(2,1)}, u32[]{:S(2)}) copy-start(bf16[128,1536]{1,0:T(8,128)(2,1)} %param.5) | copy-start | bytes 1179652
  199.7 10.3 %copy-start.1 = (bf16[1024,1536]{1,0:T(8,128)(2,1)S(1)}, bf16[1024,1536]{1,0:T(8,128)(2,1)}, u32[]{:S(2)}) copy-start(bf16[1024,1536]{1,0:T(8,128)(2,1)} %param.9) | copy-start | bytes 9437188
Sparse Core Ops, SparseCore 0:
  15.0 63.4 all-reduce.2
  85.7 31.8 reduce-scatter.1
  140.5 59.1 all-reduce.4
where the time goes:
time: 217 us; the launch traced here: 216 us
  waiting for transfers between devices  136 us (63%)
  matrix products  44.3 us (20%)
  blocking collectives  14.5 us (7%)
  between operations  13.8 us (6%)
  local copies, waits for them, and re-layouts  6.75 us (3%)
    psum x1, waiting for transfers between devices, body(): pre = lax.psum(partial_pre, 'mp')  63.5 us
    psum x1, waiting for transfers between devices, body(): d_hidden = lax.psum(grad_cols, 'mp')  40.6 us
    reduce_scatter x1, waiting for transfers between devices, body(): lax.psum_scatter(student_part - target_part, 'dp', scatter_dimension=0, t...  31.9 us
    dot_general x2, matrix products, contract_last(): lax.dot_general(left, right, (((1,), (1,)), ((), ())), preferred_element_...  15 us
    all_gather x1, blocking collectives, body(): piece = lax.all_gather(d_local, 'dp', axis=0, tiled=True)  14.5 us
    dot_general x1, matrix products, body(): grad_up = jnp.dot(d_pre, student_in, preferred_element_type=jnp.float32)  10.3 us
    dot_general x1, matrix products, body(): down_acc = jnp.dot(hidden, piece, preferred_element_type=jnp.float32)  8.22 us
    dot_general x2, matrix products, contract_first(): lax.dot_general(left, right, (((0,), (0,)), ((), ())), preferred_element_...  7.09 us
  transfers between devices with their start and end apart: 3, of which 3 were waited for; matrix products, arithmetic and copies ran while one was open for 9% of the time, Pallas kernels for 0%

commit v1 on v0

v1 whole, which is shorter than its diff:
```python
import functools
import math

import jax
import jax.numpy as jnp
from jax import lax
from jax.experimental import pallas as pl
from jax.experimental.pallas import tpu as pltpu
from jax.sharding import PartitionSpec as P

F32, BF16 = jnp.float32, jnp.bfloat16
BOTH_LAST = (((1,), (1,)), ((), ()))
BOTH_FIRST = (((0,), (0,)), ((), ()))
PLAIN = (((1,), (0,)), ((), ()))
ANY = pl.BlockSpec(memory_space=pl.ANY)
VMEM = pl.BlockSpec(memory_space=pltpu.VMEM)
MIB = 1 << 20


def mm(left, right, dims):
    return lax.dot_general(left, right, dims, preferred_element_type=F32)


def call(kernel, outs, out_specs, in_specs, scratch, args, flops, nbytes, aliases=None, limit=28):
    return pl.pallas_call(
        kernel,
        out_shape=outs,
        in_specs=in_specs,
        out_specs=out_specs,
        scratch_shapes=scratch,
        input_output_aliases=aliases or {},
        cost_estimate=pl.CostEstimate(flops=flops, bytes_accessed=nbytes, transcendentals=0),
        compiler_params=pltpu.CompilerParams(vmem_limit_bytes=limit * MIB),
    )(*args)


def rows_of(block, size):
    return pl.multiple_of((lax.axis_index("mp") ^ block) * size, size)


def load_ahead(copies, use, depth=2):
    for copy in copies[:depth]:
        copy.start()
    for at, copy in enumerate(copies):
        copy.wait()
        use(at)
        if at + depth < len(copies):
            copies[at + depth].start()


def rows_kernel(blocks, size, parts, w, s, *refs):
    outs, (buf, sem) = refs[: len(blocks)], refs[len(blocks):]
    step = size // parts
    copies = []
    for i, block in enumerate(blocks):
        base = rows_of(block, size)
        for p in range(parts):
            at = i * parts + p
            copies.append(pltpu.make_async_copy(
                w.at[pl.ds(base + p * step, step)], buf.at[at], sem.at[at]))

    def use(at):
        out = outs[at // parts]
        out[pl.ds((at % parts) * step, step)] = mm(buf[at], s[...], BOTH_LAST).astype(out.dtype)

    load_ahead(copies, use)


def rows_times(w, s, blocks, size, dtypes, parts=2):
    k, tokens = w.shape[1], s.shape[0]
    n = len(blocks)
    return call(
        functools.partial(rows_kernel, blocks, size, parts),
        [jax.ShapeDtypeStruct((size, tokens), dt) for dt in dtypes], [VMEM] * n, [ANY, VMEM],
        [pltpu.VMEM((n * parts, size // parts, k), w.dtype), pltpu.SemaphoreType.DMA((n * parts,))],
        (w, s), 2 * n * size * k * tokens, 2 * n * size * k)


def target_kernel(parts, t, w, out, buf, sem):
    step = w.shape[0] // parts
    copies = [pltpu.make_async_copy(w.at[pl.ds(p * step, step)], buf.at[p], sem.at[p]) for p in range(parts)]

    def use(p):
        term = mm(t[pl.ds(p * step, step)], buf[p], BOTH_FIRST)
        if p == 0:
            out[...] = -term
        else:
            out[...] -= term

    load_ahead(copies, use)


def minus_target(t, w, parts=2):
    (td, k), tokens = w.shape, t.shape[1]
    return call(
        functools.partial(target_kernel, parts), jax.ShapeDtypeStruct((tokens, k), F32), VMEM, [VMEM, ANY],
        [pltpu.VMEM((parts, td // parts, k), w.dtype), pltpu.SemaphoreType.DMA((parts,))],
        (t, w), 2 * td * k * tokens, 2 * td * k)


def student_kernel(blocks, size, split, acc, w, *refs):
    n = len(blocks)
    hid, refs = refs[:n], refs[n:]
    if split:
        send, keep, buf, sem, total = refs
    else:
        total, buf, sem = refs
    copies = [pltpu.make_async_copy(w.at[pl.ds(rows_of(b, size), size)], buf.at[i], sem.at[i])
              for i, b in enumerate(blocks)]

    def use(i):
        total[...] = (acc[...] if i == 0 else total[...]) + mm(hid[i][...], buf[i], BOTH_FIRST)

    load_ahead(copies, use)
    if split:
        half = total.shape[0] // 2
        core = lax.axis_index("dp") % 2
        keep[...] = total[pl.ds(pl.multiple_of(core * half, half), half)]
        send[...] = total[pl.ds(pl.multiple_of((1 - core) * half, half), half)].astype(send.dtype)


def student(acc, w, hid, blocks, size, split=False, send_dtype=BF16):
    (tokens, k), n = acc.shape, len(blocks)
    scratch = [pltpu.VMEM((n, size, k), w.dtype), pltpu.SemaphoreType.DMA((n,))]
    if split:
        outs = [jax.ShapeDtypeStruct((tokens // 2, k), send_dtype), jax.ShapeDtypeStruct((tokens // 2, k), F32)]
        scratch.append(pltpu.VMEM((tokens, k), F32))
    else:
        outs = [jax.ShapeDtypeStruct((tokens, k), F32)]
    return call(
        functools.partial(student_kernel, blocks, size, split), outs, [VMEM] * len(outs),
        [VMEM, ANY] + [VMEM] * n, scratch, (acc, w, *hid), 2 * n * size * k * tokens, 2 * n * size * k)


def fold_kernel(nz, keep, got, own, *sends):
    rows = own.shape[0]
    z = lax.axis_index("dp") // 2
    for r in range(nz):
        at = pl.ds(pl.multiple_of((z ^ r) * rows, rows), rows)
        total = keep[at] + got[at].astype(F32)
        if r == 0:
            own[...] = total
        else:
            sends[r - 1][...] = total.astype(sends[r - 1].dtype)


def fold(keep, got, nz, send_dtype=BF16):
    half, k = keep.shape
    rows = half // nz
    return call(
        functools.partial(fold_kernel, nz),
        [jax.ShapeDtypeStruct((rows, k), F32)] + [jax.ShapeDtypeStruct((rows, k), send_dtype)] * (nz - 1),
        [VMEM] * nz, [VMEM, VMEM], [], (keep, got), half * k, 8 * half * k)


def join_kernel(nz, own, *refs):
    half = refs[nz - 1]
    out = refs[nz]
    rows = own.shape[0]
    z, core = lax.axis_index("dp") // 2, lax.axis_index("dp") % 2
    size = half.shape[0]
    for r in range(nz):
        piece = own if r == 0 else refs[r - 1]
        out[pl.ds(pl.multiple_of(core * size + (z ^ r) * rows, rows), rows)] = piece[...]
        out[pl.ds(pl.multiple_of((1 - core) * size + (z ^ r) * rows, rows), rows)] = half[pl.ds(r * rows, rows)]


def join(pieces, half):
    nz = len(pieces)
    size, k = half.shape
    return call(
        functools.partial(join_kernel, nz), jax.ShapeDtypeStruct((2 * size, k), half.dtype),
        VMEM, [VMEM] * (nz + 1), [], (*pieces, half), 0, 8 * size * k)


def largest_step(total, limit):
    return max(d for d in range(16, limit + 1, 16) if total % d == 0)


def outer_kernel(blocks, size, parts, extra, *refs):
    n = len(blocks)
    left, refs = refs[:n], refs[n:]
    right, refs = refs[0], refs[1:]
    if extra == "teacher":
        teacher, out, proj, buf, sem = refs
    elif extra == "alias":
        _, out, buf, sem = refs
    else:
        out, buf, sem = refs
    step = size // parts
    slots = buf.shape[0]
    jobs = [(left[i], p * step, step, out, rows_of(b, size) + p * step, False)
            for i, b in enumerate(blocks) for p in range(parts)]
    if extra == "teacher":
        total = proj.shape[0]
        short = largest_step(total, step)
        jobs += [(teacher, p, short, proj, p, True) for p in range(0, total, short)]
    copies = []
    for at, (src, start, count, dst, row, minus) in enumerate(jobs):
        slot = at % slots
        if at >= slots:
            copies[at - slots].wait()
        term = mm(src[pl.ds(start, count)], right[...], PLAIN)
        buf[slot, pl.ds(0, count)] = -term if minus else term
        copies.append(pltpu.make_async_copy(
            buf.at[slot, pl.ds(0, count)], dst.at[pl.ds(row, count)], sem.at[slot]))
        copies[at].start()
    for copy in copies[max(0, len(jobs) - slots):]:
        copy.wait()


def outer(left, right, blocks, size, rows, teacher=None, into=None, parts=2, slots=4):
    k, n = right.shape[1], len(blocks)
    step = size // parts
    outs = [jax.ShapeDtypeStruct((rows, k), F32)]
    args, aliases, extra, done = [*left, right], {}, "", n * size
    specs = [VMEM] * (n + 1)
    if teacher is not None:
        extra = "teacher"
        outs.append(jax.ShapeDtypeStruct((teacher.shape[0], k), F32))
        args.append(teacher)
        specs.append(VMEM)
        done += teacher.shape[0]
    elif into is not None:
        extra = "alias"
        aliases = {len(args): 0}
        args.append(into)
        specs.append(ANY)
    slots = min(slots, done // step)
    return call(
        functools.partial(outer_kernel, blocks, size, parts, extra), outs, [ANY] * len(outs), specs,
        [pltpu.VMEM((slots, step, k), F32), pltpu.SemaphoreType.DMA((slots,))],
        args, 2 * done * k * right.shape[0], 4 * done * k, aliases)


def fast_body(n_mp, n_dp, student_in, teacher_hidden, w_up, w_down, w_proj):
    tokens = student_in.shape[0]
    rows = w_up.shape[0]
    size = rows // n_mp
    nz = n_dp // 2
    others = list(range(n_mp - 1, 0, -1))

    def to(x, axis, n, r):
        return lax.ppermute(x, axis, [(i, i ^ r) for i in range(n)])

    def mp(x, r):
        return to(x, "mp", n_mp, r)

    def reduce_blocks(w, s):
        got = {}
        first, *rest = others
        (x,) = rows_times(w, s, [first], size, [BF16])
        got[first] = mp(x, first)
        if rest:
            for r, x in zip(rest, rows_times(w, s, rest, size, [BF16] * len(rest))):
                got[r] = mp(x, r)
        (own,) = rows_times(w, s, [0], size, [F32])
        return own, got

    def spread(x):
        return [x] + [mp(x, r) for r in range(1, n_mp)]

    own, got = reduce_blocks(w_up, student_in)
    acc = minus_target(teacher_hidden, w_proj)
    pre = own
    for r in sorted(got):
        pre = pre + got[r].astype(F32)
    active = jnp.maximum(pre, 0.0)
    hidden = spread((active * active).astype(BF16))
    (acc,) = student(acc, w_down, hidden[:1], [0], size)
    if n_mp > 2:
        (acc,) = student(acc, w_down, hidden[1:-1], list(range(1, n_mp - 1)), size)
    send, keep = student(acc, w_down, hidden[-1:], [n_mp - 1], size, split=True)
    half = to(send, "dp", n_dp, 1)
    own, *sends = fold(keep, half, nz)
    residual = own
    for r in range(1, nz):
        residual = residual + to(sends[r - 1], "dp", n_dp, 2 * r).astype(F32)
    d_local = (residual * (1.0 / math.sqrt(tokens))).astype(BF16)
    pieces = [d_local] + [to(d_local, "dp", n_dp, 2 * r) for r in range(1, nz)]
    d_out = join(pieces, to(jnp.concatenate(pieces, 0), "dp", n_dp, 1))

    own, got = reduce_blocks(w_down, d_out)
    grad_down, grad_proj = outer(hidden, d_out, list(range(n_mp)), size, rows, teacher=teacher_hidden)
    d_hidden = own
    for r in sorted(got):
        d_hidden = d_hidden + got[r].astype(F32)
    d_pre = spread((d_hidden * (2.0 * active)).astype(BF16))
    (grad_up,) = outer(d_pre[:1], student_in, [0], size, rows)
    if n_mp > 2:
        (grad_up,) = outer(d_pre[1:-1], student_in, list(range(1, n_mp - 1)), size, rows, into=grad_up)
    (grad_up,) = outer(d_pre[-1:], student_in, [n_mp - 1], size, rows, into=grad_up)
    return grad_up, grad_down, grad_proj


def plain_body(student_in, teacher_hidden, w_up, w_down, w_proj):
    tokens = student_in.shape[0]
    pre = lax.psum(mm(w_up, student_in, BOTH_LAST), "mp")
    active = jnp.maximum(pre, 0.0)
    hidden = (active * active).astype(BF16)
    part = mm(hidden, w_down, BOTH_FIRST) - mm(teacher_hidden, w_proj, BOTH_FIRST)
    residual = lax.psum_scatter(part, "dp", scatter_dimension=0, tiled=True)
    d_local = (residual * (1.0 / math.sqrt(tokens))).astype(BF16)
    d_out = lax.all_gather(d_local, "dp", axis=0, tiled=True)
    grad_down = mm(hidden, d_out, PLAIN)
    grad_proj = -mm(teacher_hidden, d_out, PLAIN)
    d_hidden = lax.psum(mm(w_down, d_out, BOTH_LAST), "mp")
    d_pre = (d_hidden * (2.0 * active)).astype(BF16)
    grad_up = mm(d_pre, student_in, PLAIN)
    return grad_up, grad_down, grad_proj


def solution(mesh):
    n_mp, n_dp = mesh.shape["mp"], mesh.shape["dp"]

    def body(student_in, teacher_hidden, w_up, w_down, w_proj):
        tokens, size = student_in.shape[0], w_up.shape[0] // n_mp
        fits = (
            n_mp in (2, 4, 8) and n_dp in (2, 4, 8, 16)
            and w_up.shape[0] % n_mp == 0 and size % 64 == 0
            and tokens % (16 * n_dp) == 0 and student_in.shape[1] % 128 == 0
            and teacher_hidden.shape[0] % 32 == 0
        )
        args = (student_in, teacher_hidden, w_up, w_down, w_proj)
        return fast_body(n_mp, n_dp, *args) if fits else plain_body(*args)

    return jax.shard_map(
        body,
        mesh=mesh,
        in_specs=(P(None, "mp"), P("dp", None), P("dp", "mp"), P("dp", "mp"), P("dp", "mp")),
        out_specs=(P("dp", "mp"), P("dp", "mp"), P("dp", "mp")),
        check_vma=False,
    )
```

time: 217 us -> 94.6 us (0.44)
  waiting for transfers between devices: 136 us -> 25.6 us
  matrix products: 44.3 us -> 0 us
  Pallas kernels: 0 us -> 38.4 us
  starting transfers between devices: 0.12 us -> 24.4 us
  blocking collectives: 14.5 us -> 0 us
  between operations: 13.8 us -> 1.05 us
    psum x2 -> x0, waiting for transfers between devices: 104 us -> none  [the longest x1 63.5 us: body(): pre = lax.psum(partial_pre, 'mp')]
    dot_general x7 -> x0, matrix products: 44.3 us -> none  [the longest x2 15 us: contract_last(): lax.dot_general(left, right, (((1,), (1,)), ((), ())), preferred_element_...]
    pallas_call x0 -> x16, Pallas kernels: none -> 38.4 us  [call(): pl.pallas_call(kernel, out_shape=outs, in_specs=in_specs, out_specs=out_s...]
    reduce_scatter x1 -> x0, waiting for transfers between devices: 31.9 us -> none  [body(): lax.psum_scatter(student_part - target_part, 'dp', scatter_dimension=0, t...]
    ppermute x0 -> x20, waiting for transfers between devices: none -> 25.6 us  [to(): return lax.ppermute(x, axis, [(i, i ^ r) for i in range(n)])]
    ppermute x0 -> x20, starting transfers between devices: none -> 24.4 us  [to(): return lax.ppermute(x, axis, [(i, i ^ r) for i in range(n)])]
    all_gather x1 -> x0, blocking collectives: 14.5 us -> none  [body(): piece = lax.all_gather(d_local, 'dp', axis=0, tiled=True)]
    unnamed x11 -> x16, local copies, waits for them, and re-layouts: 6.75 us -> 4.7 us
  transfers between devices with their start and end apart: 3 -> 20, of which waited for: 3 -> 13; matrix products, arithmetic and copies ran while one was open for 9% -> 0% of each run, Pallas kernels for 0% -> 28%
where the time goes in v1:
time: 94.6 us; the launch traced here: 94.4 us
  Pallas kernels  38.4 us (41%)
  waiting for transfers between devices  25.6 us (27%)
  starting transfers between devices  24.4 us (26%)
  local copies, waits for them, and re-layouts  4.7 us (5%)
  between operations  1.05 us (1%)
    pallas_call x16, Pallas kernels, call(): pl.pallas_call(kernel, out_shape=outs, in_specs=in_specs, out_specs=out_s...  38.4 us
    ppermute x20, waiting for transfers between devices, to(): return lax.ppermute(x, axis, [(i, i ^ r) for i in range(n)])  25.6 us
    ppermute x20, starting transfers between devices, to(): return lax.ppermute(x, axis, [(i, i ^ r) for i in range(n)])  24.4 us
    unnamed x16, local copies, waits for them, and re-layouts  4.7 us
  transfers between devices with their start and end apart: 20, of which 13 were waited for; matrix products, arithmetic and copies ran while one was open for 0% of the time, Pallas kernels for 28%

profile of v1, /device:TPU:0, one launch (start us, length us, event | category | flops | bytes accessed | tf_op | source)
XLA Modules:
  0.0 94.4 jit_solution(3009003124499034254)
XLA Ops:
  0.6 0.0 copy-start
  0.6 3.7 %copy-done = bf16[3072,1536]{1,0:T(8,128)(2,1)S(1)} copy-done((bf16[3072,1536]{1,0:T(8,128)(2,1)S(1)}, bf16[3072,1536]{1,0:T(8,128)(2,1)}, u32[]{:S(2)}) %copy-start) | copy-done | bytes 9437208
  4.3 1.0 %copy-done.1 = bf16[128,1536]{1,0:T(8,128)(2,1)S(1)} copy-done((bf16[128,1536]{1,0:T(8,128)(2,1)S(1)}, bf16[128,1536]{1,0:T(8,128)(2,1)}, u32[]{:S(2)}) %copy-start.1) | copy-done | bytes 393240
  5.3 2.0 %shard_map.79 = bf16[768,128]{1,0:T(8,128)(2,1)S(1)} custom-call(bf16[3072,1536]{1,0:T(8,128)(2,1)S(1)} %copy-done, bf16[128,1536]{1,0:T(8,128)(2,1)S(1)} %copy-done.1), custom_call_target="tpu_custom_call" | custom-call | flops 301989888 | bytes 2359296 | tf_op jit(solution)/shard_map/pallas_call | solution.py:25
  7.3 0.0 slice-start.1
  7.3 4.0 %collective-permute-start.2 = (bf16[768,128]{1,0:T(8,128)(2,1)S(1)}, bf16[768,128]{1,0:T(8,128)(2,1)S(1)}, u32[]{:S(2)}, u32[]{:S(2)}) collective-permute-start(bf16[768,128]{1,0:T(8,128)(2,1)S(1)} %shard_map.79), channel_id=1, source_target_pairs={{0,3},{1,2},{2,1},{3,0},{4,7},{5,6},{6,5},{7,4},{8,11},{9,10},{10,... | collective-permute-start | bytes 589832 | tf_op jit(solution)/shard_map/ppermute | solution.py:244
  11.3 4.0 %shard_map.78 = (bf16[768,128]{1,0:T(8,128)(2,1)S(1)}, bf16[768,128]{1,0:T(8,128)(2,1)S(1)}) custom-call(bf16[3072,1536]{1,0:T(8,128)(2,1)S(1)} %copy-done, bf16[128,1536]{1,0:T(8,128)(2,1)S(1)} %copy-done.1), custom_call_target="tpu_custom_call" | custom-call | flops 603979776 | bytes 4718592 | tf_op jit(solution)/shard_map/pallas_call | solution.py:25
  15.3 0.6 collective-permute-start
  15.9 0.1 collective-permute-start.1
  16.0 2.0 %shard_map.77 = f32[768,128]{1,0:T(8,128)S(1)} custom-call(bf16[3072,1536]{1,0:T(8,128)(2,1)S(1)} %copy-done, bf16[128,1536]{1,0:T(8,128)(2,1)S(1)} %copy-done.1), custom_call_target="tpu_custom_call" | custom-call | flops 301989888 | bytes 2359296 | tf_op jit(solution)/shard_map/pallas_call | solution.py:25
  18.0 0.0 collective-permute-done.2
  18.0 3.7 %collective-permute-done = bf16[768,128]{1,0:T(8,128)(2,1)S(1)} collective-permute-done((bf16[768,128]{1,0:T(8,128)(2,1)S(1)}, bf16[768,128]{1,0:T(8,128)(2,1)S(1)}, u32[]{:S(2)}, u32[]{:S(2)}) %collective-permute-start) | collective-permute-done | bytes 196640 | tf_op jit(solution)/shard_map/ppermute | solution.py:244
  21.8 0.3 collective-permute-done.1
  22.0 0.1 multiply_convert_fusion.1.refs_0_
  22.1 0.4 collective-permute-start.4
  22.6 1.7 %collective-permute-start.3 = (bf16[768,128]{1,0:T(8,128)(2,1)S(1)}, bf16[768,128]{1,0:T(8,128)(2,1)S(1)}, u32[]{:S(2)}, u32[]{:S(2)}) collective-permute-start(bf16[768,128]{1,0:T(8,128)(2,1)S(1)} %multiply_convert_fusion.1.refs_0_), channel_id=1, source_target_pairs={{0,1},{1,0},{2,3},{3,2},{4,5},{5,4},{6,7},{7,6},{8,9},{9,8},{10,11... | collective-permute-start | bytes 589832 | tf_op jit(solution)/shard_map/ppermute | solution.py:244
  24.2 1.5 %collective-permute-start.5 = (bf16[768,128]{1,0:T(8,128)(2,1)S(1)}, bf16[768,128]{1,0:T(8,128)(2,1)S(1)}, u32[]{:S(2)}, u32[]{:S(2)}) collective-permute-start(bf16[768,128]{1,0:T(8,128)(2,1)S(1)} %multiply_convert_fusion.1.refs_0_), channel_id=1, source_target_pairs={{0,3},{1,2},{2,1},{3,0},{4,7},{5,6},{6,5},{7,4},{8,11},{9,10},{10,... | collective-permute-start | bytes 589832 | tf_op jit(solution)/shard_map/ppermute | solution.py:244
  25.7 1.0 %shard_map.76.acc = f32[128,1536]{1,0:T(8,128)S(1)} custom-call(bf16[1024,128]{1,0:T(8,128)(2,1)S(1)} %copy-done.4, bf16[1024,1536]{1,0:T(8,128)(2,1)S(1)} %copy-done.3), custom_call_target="tpu_custom_call" | custom-call | flops 402653184 | bytes 3145728 | tf_op jit(solution)/shard_map/pallas_call | solution.py:25
  26.7 0.0 slice-done
  26.8 0.0 slice-done.1
  26.8 0.0 slice-done.2
  26.8 0.7 shard_map.80.acc
  27.5 2.5 %collective-permute-done.4.refs_1_.refs_2_ = bf16[768,128]{1,0:T(8,128)(2,1)S(1)} collective-permute-done((bf16[768,128]{1,0:T(8,128)(2,1)S(1)}, bf16[768,128]{1,0:T(8,128)(2,1)S(1)}, u32[]{:S(2)}, u32[]{:S(2)}) %collective-permute-start.4) | collective-permute-done | bytes 196640 | tf_op jit(solution)/shard_map/ppermute | solution.py:244
  29.9 0.0 collective-permute-done.3.refs_0_.refs_1_
  29.9 1.3 %shard_map.81.acc = f32[128,1536]{1,0:T(8,128)S(1)} custom-call(f32[128,1536]{1,0:T(8,128)S(1)} %shard_map.80.acc, bf16[3072,1536]{1,0:T(8,128)(2,1)S(1)} %bitcast.1, bf16[768,128]{1,0:T(8,128)(2,1)S(1)} %collective-permute-done.3.refs_0_.refs_1_, bf16[768,128]{1,0:T(8,128)(2,1)S(1)} %collective-permute-done.4.refs_1_.refs_2_), custom_call_target="tpu_custom_call" | custom-call | flops 603979776 | bytes 4718592 | tf_op jit(solution)/shard_map/pallas_call | solution.py:25
  31.2 1.7 %collective-permute-done.5.refs_0_.refs_3_ = bf16[768,128]{1,0:T(8,128)(2,1)S(1)} collective-permute-done((bf16[768,128]{1,0:T(8,128)(2,1)S(1)}, bf16[768,128]{1,0:T(8,128)(2,1)S(1)}, u32[]{:S(2)}, u32[]{:S(2)}) %collective-permute-start.5) | collective-permute-done | bytes 196640 | tf_op jit(solution)/shard_map/ppermute | solution.py:244
  32.9 0.8 shard_map.82
  33.6 0.1 collective-permute-start.6
  33.7 1.4 %collective-permute-done.6.got = bf16[64,1536]{1,0:T(8,128)(2,1)S(1)} collective-permute-done((bf16[64,1536]{1,0:T(8,128)(2,1)S(1)}, bf16[64,1536]{1,0:T(8,128)(2,1)S(1)}, u32[]{:S(2)}, u32[]{:S(2)}) %collective-permute-start.6) | collective-permute-done | bytes 196640 | tf_op jit(solution)/shard_map/ppermute | solution.py:244
  35.2 1.6 %collective-permute-start.7 = (bf16[16,1536]{1,0:T(8,128)(2,1)S(1)}, bf16[16,1536]{1,0:T(8,128)(2,1)S(1)}, u32[]{:S(2)}, u32[]{:S(2)}) collective-permute-start(bf16[16,1536]{1,0:T(8,128)(2,1)S(1)} %get-tuple-element.20), channel_id=1, source_target_pairs={{0,8},{4,12},{8,0},{12,4},{16,24},{20,28},{24,16},{28,20},{1,9},{5... | collective-permute-start | bytes 147464 | tf_op jit(solution)/shard_map/ppermute | solution.py:244
  36.8 2.6 %collective-permute-start.8 = (bf16[16,1536]{1,0:T(8,128)(2,1)S(1)}, bf16[16,1536]{1,0:T(8,128)(2,1)S(1)}, u32[]{:S(2)}, u32[]{:S(2)}) collective-permute-start(bf16[16,1536]{1,0:T(8,128)(2,1)S(1)} %get-tuple-element.21), channel_id=1, source_target_pairs={{0,16},{4,20},{8,24},{12,28},{16,0},{20,4},{24,8},{28,12},{1,17},{... | collective-permute-start | bytes 147464 | tf_op jit(solution)/shard_map/ppermute | solution.py:244
  39.4 0.2 collective-permute-start.9
  39.6 0.0 collective-permute-done.7
  39.6 3.0 %collective-permute-done.8 = bf16[16,1536]{1,0:T(8,128)(2,1)S(1)} collective-permute-done((bf16[16,1536]{1,0:T(8,128)(2,1)S(1)}, bf16[16,1536]{1,0:T(8,128)(2,1)S(1)}, u32[]{:S(2)}, u32[]{:S(2)}) %collective-permute-start.8) | collective-permute-done | bytes 49184 | tf_op jit(solution)/shard_map/ppermute | solution.py:244
  42.7 2.6 %collective-permute-done.9 = bf16[16,1536]{1,0:T(8,128)(2,1)S(1)} collective-permute-done((bf16[16,1536]{1,0:T(8,128)(2,1)S(1)}, bf16[16,1536]{1,0:T(8,128)(2,1)S(1)}, u32[]{:S(2)}, u32[]{:S(2)}) %collective-permute-start.9) | collective-permute-done | bytes 49184 | tf_op jit(solution)/shard_map/ppermute | solution.py:244
  45.3 1.1 %collective-permute-start.12 = (bf16[16,1536]{1,0:T(8,128)(2,1)S(1)}, bf16[16,1536]{1,0:T(8,128)(2,1)S(1)}, u32[]{:S(2)}, u32[]{:S(2)}) collective-permute-start(bf16[16,1536]{1,0:T(8,128)(2,1)S(1)} %multiply_convert_fusion.2.own), channel_id=1, source_target_pairs={{0,24},{4,28},{8,16},{12,20},{16,8},{20,12},{24,0},{28,4},{1,25},{... | collective-permute-start | bytes 147464 | tf_op jit(solution)/shard_map/ppermute | solution.py:244
  46.4 0.0 collective-permute-start.11
  46.4 3.3 %collective-permute-start.10 = (bf16[16,1536]{1,0:T(8,128)(2,1)S(1)}, bf16[16,1536]{1,0:T(8,128)(2,1)S(1)}, u32[]{:S(2)}, u32[]{:S(2)}) collective-permute-start(bf16[16,1536]{1,0:T(8,128)(2,1)S(1)} %multiply_convert_fusion.2.own), channel_id=1, source_target_pairs={{0,8},{4,12},{8,0},{12,4},{16,24},{20,28},{24,16},{28,20},{1,9},{5... | collective-permute-start | bytes 147464 | tf_op jit(solution)/shard_map/ppermute | solution.py:244
  49.8 1.5 %collective-permute-done.12.refs_2_ = bf16[16,1536]{1,0:T(8,128)(2,1)S(1)} collective-permute-done((bf16[16,1536]{1,0:T(8,128)(2,1)S(1)}, bf16[16,1536]{1,0:T(8,128)(2,1)S(1)}, u32[]{:S(2)}, u32[]{:S(2)}) %collective-permute-start.12) | collective-permute-done | bytes 49184 | tf_op jit(solution)/shard_map/ppermute | solution.py:244
  51.3 1.0 %collective-permute-done.11.refs_1_ = bf16[16,1536]{1,0:T(8,128)(2,1)S(1)} collective-permute-done((bf16[16,1536]{1,0:T(8,128)(2,1)S(1)}, bf16[16,1536]{1,0:T(8,128)(2,1)S(1)}, u32[]{:S(2)}, u32[]{:S(2)}) %collective-permute-start.11) | collective-permute-done | bytes 49184 | tf_op jit(solution)/shard_map/ppermute | solution.py:244
  52.3 0.0 collective-permute-done.10.refs_0_
  52.4 0.1 collective-permute-start.13
  52.4 1.4 %collective-permute-done.13.refs_3_ = bf16[64,1536]{1,0:T(8,128)(2,1)S(1)} collective-permute-done((bf16[64,1536]{1,0:T(8,128)(2,1)S(1)}, bf16[64,1536]{1,0:T(8,128)(2,1)S(1)}, u32[]{:S(2)}, u32[]{:S(2)}) %collective-permute-start.13) | collective-permute-done | bytes 196640 | tf_op jit(solution)/shard_map/ppermute | solution.py:244
  53.9 0.0 copy-start.2
  53.9 2.0 %shard_map.87 = bf16[768,128]{1,0:T(8,128)(2,1)S(1)} custom-call(bf16[3072,1536]{1,0:T(8,128)(2,1)S(1)} %bitcast.1, bf16[128,1536]{1,0:T(8,128)(2,1)S(1)} %shard_map.84.s.refs_4_), custom_call_target="tpu_custom_call" | custom-call | flops 301989888 | bytes 2359296 | tf_op jit(solution)/shard_map/pallas_call | solution.py:25
  56.0 4.0 %shard_map.86 = (bf16[768,128]{1,0:T(8,128)(2,1)S(1)}, bf16[768,128]{1,0:T(8,128)(2,1)S(1)}) custom-call(bf16[3072,1536]{1,0:T(8,128)(2,1)S(1)} %bitcast.1, bf16[128,1536]{1,0:T(8,128)(2,1)S(1)} %shard_map.84.s.refs_4_), custom_call_target="tpu_custom_call" | custom-call | flops 603979776 | bytes 4718592 | tf_op jit(solution)/shard_map/pallas_call | solution.py:25
  60.0 1.5 %collective-permute-start.16 = (bf16[768,128]{1,0:T(8,128)(2,1)S(1)}, bf16[768,128]{1,0:T(8,128)(2,1)S(1)}, u32[]{:S(2)}, u32[]{:S(2)}) collective-permute-start(bf16[768,128]{1,0:T(8,128)(2,1)S(1)} %shard_map.87), channel_id=1, source_target_pairs={{0,3},{1,2},{2,1},{3,0},{4,7},{5,6},{6,5},{7,4},{8,11},{9,10},{10,... | collective-permute-start | bytes 589832 | tf_op jit(solution)/shard_map/ppermute | solution.py:244
  61.5 0.6 collective-permute-start.14
  62.1 1.5 %collective-permute-start.15 = (bf16[768,128]{1,0:T(8,128)(2,1)S(1)}, bf16[768,128]{1,0:T(8,128)(2,1)S(1)}, u32[]{:S(2)}, u32[]{:S(2)}) collective-permute-start(bf16[768,128]{1,0:T(8,128)(2,1)S(1)} %get-tuple-element.24), channel_id=1, source_target_pairs={{0,2},{1,3},{2,0},{3,1},{4,6},{5,7},{6,4},{7,5},{8,10},{9,11},{10,... | collective-permute-start | bytes 589832 | tf_op jit(solution)/shard_map/ppermute | solution.py:244
  63.5 2.2 %shard_map.85 = f32[768,128]{1,0:T(8,128)S(1)} custom-call(bf16[3072,1536]{1,0:T(8,128)(2,1)S(1)} %bitcast.1, bf16[128,1536]{1,0:T(8,128)(2,1)S(1)} %shard_map.84.s.refs_4_), custom_call_target="tpu_custom_call" | custom-call | flops 301989888 | bytes 2359296 | tf_op jit(solution)/shard_map/pallas_call | solution.py:25
  65.7 3.0 %collective-permute-done.16 = bf16[768,128]{1,0:T(8,128)(2,1)S(1)} collective-permute-done((bf16[768,128]{1,0:T(8,128)(2,1)S(1)}, bf16[768,128]{1,0:T(8,128)(2,1)S(1)}, u32[]{:S(2)}, u32[]{:S(2)}) %collective-permute-start.16) | collective-permute-done | bytes 196640 | tf_op jit(solution)/shard_map/ppermute | solution.py:244
  68.8 2.5 %collective-permute-done.14 = bf16[768,128]{1,0:T(8,128)(2,1)S(1)} collective-permute-done((bf16[768,128]{1,0:T(8,128)(2,1)S(1)}, bf16[768,128]{1,0:T(8,128)(2,1)S(1)}, u32[]{:S(2)}, u32[]{:S(2)}) %collective-permute-start.14) | collective-permute-done | bytes 196640 | tf_op jit(solution)/shard_map/ppermute | solution.py:244
  71.2 0.9 collective-permute-done.15
  72.1 0.2 multiply_convert_fusion.refs_0_
  72.3 0.7 collective-permute-start.19
  73.0 1.5 %collective-permute-start.18 = (bf16[768,128]{1,0:T(8,128)(2,1)S(1)}, bf16[768,128]{1,0:T(8,128)(2,1)S(1)}, u32[]{:S(2)}, u32[]{:S(2)}) collective-permute-start(bf16[768,128]{1,0:T(8,128)(2,1)S(1)} %multiply_convert_fusion.refs_0_), channel_id=1, source_target_pairs={{0,1},{1,0},{2,3},{3,2},{4,5},{5,4},{6,7},{7,6},{8,9},{9,8},{10,11... | collective-permute-start | bytes 589832 | tf_op jit(solution)/shard_map/ppermute | solution.py:244
  74.5 1.4 %collective-permute-start.17 = (bf16[768,128]{1,0:T(8,128)(2,1)S(1)}, bf16[768,128]{1,0:T(8,128)(2,1)S(1)}, u32[]{:S(2)}, u32[]{:S(2)}) collective-permute-start(bf16[768,128]{1,0:T(8,128)(2,1)S(1)} %multiply_convert_fusion.refs_0_), channel_id=1, source_target_pairs={{0,3},{1,2},{2,1},{3,0},{4,7},{5,6},{6,5},{7,4},{8,11},{9,10},{10,... | collective-permute-start | bytes 589832 | tf_op jit(solution)/shard_map/ppermute | solution.py:244
  75.9 8.9 %shard_map.91 = (f32[3072,1536]{1,0:T(8,128)}, f32[1024,1536]{1,0:T(8,128)}) custom-call(bf16[768,128]{1,0:T(8,128)(2,1)S(1)} %multiply_convert_fusion.1.refs_0_, bf16[768,128]{1,0:T(8,128)(2,1)S(1)} %collective-permute-done.3.refs_0_.refs_1_, bf16[768,128]{1,0:T(8,128)(2,1)S(1)} %collective-permute-done.4.refs_1_.refs_2_, ...), custom_call_target="tpu_custom_call" | custom-call | flops 1610612736 | bytes 25165824 | tf_op jit(solution)/shard_map/pallas_call | solution.py:25
  84.8 2.7 %shard_map.88.refs_3_ = f32[3072,1536]{1,0:T(8,128)} custom-call(bf16[768,128]{1,0:T(8,128)(2,1)S(1)} %multiply_convert_fusion.refs_0_, bf16[128,1536]{1,0:T(8,128)(2,1)S(1)} %copy-done.2), custom_call_target="tpu_custom_call" | custom-call | flops 301989888 | bytes 4718592 | tf_op jit(solution)/shard_map/pallas_call | solution.py:25
  87.4 0.0 collective-permute-done.19.refs_1_
  87.4 0.0 collective-permute-done.18.refs_0_
  87.4 4.2 %shard_map.89.refs_2_ = f32[3072,1536]{1,0:T(8,128)} custom-call(bf16[768,128]{1,0:T(8,128)(2,1)S(1)} %collective-permute-done.18.refs_0_, bf16[768,128]{1,0:T(8,128)(2,1)S(1)} %collective-permute-done.19.refs_1_, bf16[128,1536]{1,0:T(8,128)(2,1)S(1)} %copy-done.2, f32[3072,1536]{1,0:T(8,128)} %shard_map.88.refs_3_), custom_call_target="tpu_custom_call", output_to_operand_aliasing={{}: (3, {})} | custom-call | flops 603979776 | bytes 9437184 | tf_op jit(solution)/shard_map/pallas_call | solution.py:25
  91.6 0.0 collective-permute-done.17.refs_0_
  91.6 2.7 %shard_map.90 = f32[3072,1536]{1,0:T(8,128)} custom-call(bf16[768,128]{1,0:T(8,128)(2,1)S(1)} %collective-permute-done.17.refs_0_, bf16[128,1536]{1,0:T(8,128)(2,1)S(1)} %copy-done.2, f32[3072,1536]{1,0:T(8,128)} %shard_map.89.refs_2_), custom_call_target="tpu_custom_call", output_to_operand_aliasing={{}: (2, {})} | custom-call | flops 301989888 | bytes 4718592 | tf_op jit(solution)/shard_map/pallas_call | solution.py:25
  (13 shorter events, 0.1 us)
Async XLA Ops:
  0.6 3.7 %copy-start = (bf16[3072,1536]{1,0:T(8,128)(2,1)S(1)}, bf16[3072,1536]{1,0:T(8,128)(2,1)}, u32[]{:S(2)}) copy-start(bf16[3072,1536]{1,0:T(8,128)(2,1)} %w.13) | copy-start | bytes 28311556
  4.3 1.0 %copy-start.1 = (bf16[128,1536]{1,0:T(8,128)(2,1)S(1)}, bf16[128,1536]{1,0:T(8,128)(2,1)}, u32[]{:S(2)}) copy-start(bf16[128,1536]{1,0:T(8,128)(2,1)} %refs_1_.3) | copy-start | bytes 1179652
  5.3 20.4 %copy-start.3 = (bf16[1024,1536]{1,0:T(8,128)(2,1)S(1)}, bf16[1024,1536]{1,0:T(8,128)(2,1)}, u32[]{:S(2)}) copy-start(bf16[1024,1536]{1,0:T(8,128)(2,1)} %w.10) | copy-start | bytes 9437188
  5.3 20.4 %copy-start.4 = (bf16[1024,128]{1,0:T(8,128)(2,1)S(1)}, bf16[1024,128]{1,0:T(8,128)(2,1)}, u32[]{:S(2)}) copy-start(bf16[1024,128]{1,0:T(8,128)(2,1)} %refs_5_.1) | copy-start | bytes 786436
  5.3 21.4 %slice-start = ((s8[9437184]{0:T(1024)(128)(4,1)}), s8[4194304]{0:T(1024)(128)(4,1)S(1)}, s32[]{:S(2)}) async-start(s8[9437184]{0:T(1024)(128)(4,1)} %bitcast), calls=%async_computation | async-start | bytes 8388608
  7.3 19.4 %slice-start.1 = ((s8[9437184]{0:T(1024)(128)(4,1)}), s8[4194304]{0:T(1024)(128)(4,1)S(1)}, s32[]{:S(2)}) async-start(s8[9437184]{0:T(1024)(128)(4,1)} %bitcast), calls=%async_computation.1 | async-start | bytes 8388608
  7.3 10.7 %collective-permute-start.2 = (bf16[768,128]{1,0:T(8,128)(2,1)S(1)}, bf16[768,128]{1,0:T(8,128)(2,1)S(1)}, u32[]{:S(2)}, u32[]{:S(2)}) collective-permute-start(bf16[768,128]{1,0:T(8,128)(2,1)S(1)} %shard_map.79), channel_id=1, source_target_pairs={{0,3},{1,2},{2,1},{3,0},{4,7},{5,6},{6,5},{7,4},{8,11},{9,10},{10,... | collective-permute-start | bytes 589832 | tf_op jit(solution)/shard_map/ppermute | solution.py:244
  15.3 6.4 %collective-permute-start = (bf16[768,128]{1,0:T(8,128)(2,1)S(1)}, bf16[768,128]{1,0:T(8,128)(2,1)S(1)}, u32[]{:S(2)}, u32[]{:S(2)}) collective-permute-start(bf16[768,128]{1,0:T(8,128)(2,1)S(1)} %get-tuple-element.15), channel_id=1, source_target_pairs={{0,1},{1,0},{2,3},{3,2},{4,5},{5,4},{6,7},{7,6},{8,9},{9,8},{10,11... | collective-permute-start | bytes 589832 | tf_op jit(solution)/shard_map/ppermute | solution.py:244
  15.9 10.8 %slice-start.2 = ((s8[9437184]{0:T(1024)(128)(4,1)}), s8[1048576]{0:T(1024)(128)(4,1)S(1)}, s32[]{:S(2)}) async-start(s8[9437184]{0:T(1024)(128)(4,1)} %bitcast), calls=%async_computation.2 | async-start | bytes 2097152
  15.9 6.1 %collective-permute-start.1 = (bf16[768,128]{1,0:T(8,128)(2,1)S(1)}, bf16[768,128]{1,0:T(8,128)(2,1)S(1)}, u32[]{:S(2)}, u32[]{:S(2)}) collective-permute-start(bf16[768,128]{1,0:T(8,128)(2,1)S(1)} %get-tuple-element.16), channel_id=1, source_target_pairs={{0,2},{1,3},{2,0},{3,1},{4,6},{5,7},{6,4},{7,5},{8,10},{9,11},{10,... | collective-permute-start | bytes 589832 | tf_op jit(solution)/shard_map/ppermute | solution.py:244
  22.1 7.8 %collective-permute-start.4 = (bf16[768,128]{1,0:T(8,128)(2,1)S(1)}, bf16[768,128]{1,0:T(8,128)(2,1)S(1)}, u32[]{:S(2)}, u32[]{:S(2)}) collective-permute-start(bf16[768,128]{1,0:T(8,128)(2,1)S(1)} %multiply_convert_fusion.1.refs_0_), channel_id=1, source_target_pairs={{0,2},{1,3},{2,0},{3,1},{4,6},{5,7},{6,4},{7,5},{8,10},{9,11},{10,... | collective-permute-start | bytes 589832 | tf_op jit(solution)/shard_map/ppermute | solution.py:244
  22.6 7.4 %collective-permute-start.3 = (bf16[768,128]{1,0:T(8,128)(2,1)S(1)}, bf16[768,128]{1,0:T(8,128)(2,1)S(1)}, u32[]{:S(2)}, u32[]{:S(2)}) collective-permute-start(bf16[768,128]{1,0:T(8,128)(2,1)S(1)} %multiply_convert_fusion.1.refs_0_), channel_id=1, source_target_pairs={{0,1},{1,0},{2,3},{3,2},{4,5},{5,4},{6,7},{7,6},{8,9},{9,8},{10,11... | collective-permute-start | bytes 589832 | tf_op jit(solution)/shard_map/ppermute | solution.py:244
  24.2 8.6 %collective-permute-start.5 = (bf16[768,128]{1,0:T(8,128)(2,1)S(1)}, bf16[768,128]{1,0:T(8,128)(2,1)S(1)}, u32[]{:S(2)}, u32[]{:S(2)}) collective-permute-start(bf16[768,128]{1,0:T(8,128)(2,1)S(1)} %multiply_convert_fusion.1.refs_0_), channel_id=1, source_target_pairs={{0,3},{1,2},{2,1},{3,0},{4,7},{5,6},{6,5},{7,4},{8,11},{9,10},{10,... | collective-permute-start | bytes 589832 | tf_op jit(solution)/shard_map/ppermute | solution.py:244
  33.6 1.5 %collective-permute-start.6 = (bf16[64,1536]{1,0:T(8,128)(2,1)S(1)}, bf16[64,1536]{1,0:T(8,128)(2,1)S(1)}, u32[]{:S(2)}, u32[]{:S(2)}) collective-permute-start(bf16[64,1536]{1,0:T(8,128)(2,1)S(1)} %get-tuple-element.18), channel_id=1, source_target_pairs={{0,4},{4,0},{8,12},{12,8},{16,20},{20,16},{24,28},{28,24},{1,5},{5... | collective-permute-start | bytes 589832 | tf_op jit(solution)/shard_map/ppermute | solution.py:244
  35.2 4.5 %collective-permute-start.7 = (bf16[16,1536]{1,0:T(8,128)(2,1)S(1)}, bf16[16,1536]{1,0:T(8,128)(2,1)S(1)}, u32[]{:S(2)}, u32[]{:S(2)}) collective-permute-start(bf16[16,1536]{1,0:T(8,128)(2,1)S(1)} %get-tuple-element.20), channel_id=1, source_target_pairs={{0,8},{4,12},{8,0},{12,4},{16,24},{20,28},{24,16},{28,20},{1,9},{5... | collective-permute-start | bytes 147464 | tf_op jit(solution)/shard_map/ppermute | solution.py:244
  36.8 5.8 %collective-permute-start.8 = (bf16[16,1536]{1,0:T(8,128)(2,1)S(1)}, bf16[16,1536]{1,0:T(8,128)(2,1)S(1)}, u32[]{:S(2)}, u32[]{:S(2)}) collective-permute-start(bf16[16,1536]{1,0:T(8,128)(2,1)S(1)} %get-tuple-element.21), channel_id=1, source_target_pairs={{0,16},{4,20},{8,24},{12,28},{16,0},{20,4},{24,8},{28,12},{1,17},{... | collective-permute-start | bytes 147464 | tf_op jit(solution)/shard_map/ppermute | solution.py:244
  39.4 5.9 %collective-permute-start.9 = (bf16[16,1536]{1,0:T(8,128)(2,1)S(1)}, bf16[16,1536]{1,0:T(8,128)(2,1)S(1)}, u32[]{:S(2)}, u32[]{:S(2)}) collective-permute-start(bf16[16,1536]{1,0:T(8,128)(2,1)S(1)} %get-tuple-element.22), channel_id=1, source_target_pairs={{0,24},{4,28},{8,16},{12,20},{16,8},{20,12},{24,0},{28,4},{1,25},{... | collective-permute-start | bytes 147464 | tf_op jit(solution)/shard_map/ppermute | solution.py:244
  45.3 6.0 %collective-permute-start.12 = (bf16[16,1536]{1,0:T(8,128)(2,1)S(1)}, bf16[16,1536]{1,0:T(8,128)(2,1)S(1)}, u32[]{:S(2)}, u32[]{:S(2)}) collective-permute-start(bf16[16,1536]{1,0:T(8,128)(2,1)S(1)} %multiply_convert_fusion.2.own), channel_id=1, source_target_pairs={{0,24},{4,28},{8,16},{12,20},{16,8},{20,12},{24,0},{28,4},{1,25},{... | collective-permute-start | bytes 147464 | tf_op jit(solution)/shard_map/ppermute | solution.py:244
  46.4 5.9 %collective-permute-start.11 = (bf16[16,1536]{1,0:T(8,128)(2,1)S(1)}, bf16[16,1536]{1,0:T(8,128)(2,1)S(1)}, u32[]{:S(2)}, u32[]{:S(2)}) collective-permute-start(bf16[16,1536]{1,0:T(8,128)(2,1)S(1)} %multiply_convert_fusion.2.own), channel_id=1, source_target_pairs={{0,16},{4,20},{8,24},{12,28},{16,0},{20,4},{24,8},{28,12},{1,17},{... | collective-permute-start | bytes 147464 | tf_op jit(solution)/shard_map/ppermute | solution.py:244
  46.4 5.9 %collective-permute-start.10 = (bf16[16,1536]{1,0:T(8,128)(2,1)S(1)}, bf16[16,1536]{1,0:T(8,128)(2,1)S(1)}, u32[]{:S(2)}, u32[]{:S(2)}) collective-permute-start(bf16[16,1536]{1,0:T(8,128)(2,1)S(1)} %multiply_convert_fusion.2.own), channel_id=1, source_target_pairs={{0,8},{4,12},{8,0},{12,4},{16,24},{20,28},{24,16},{28,20},{1,9},{5... | collective-permute-start | bytes 147464 | tf_op jit(solution)/shard_map/ppermute | solution.py:244
  52.4 1.5 %collective-permute-start.13 = (bf16[64,1536]{1,0:T(8,128)(2,1)S(1)}, bf16[64,1536]{1,0:T(8,128)(2,1)S(1)}, u32[]{:S(2)}, u32[]{:S(2)}) collective-permute-start(bf16[64,1536]{1,0:T(8,128)(2,1)S(1)} %pad_maximum_fusion), channel_id=1, source_target_pairs={{0,4},{4,0},{8,12},{12,8},{16,20},{20,16},{24,28},{28,24},{1,5},{5... | collective-permute-start | bytes 589832 | tf_op jit(solution)/shard_map/ppermute | solution.py:244
  53.9 30.8 %copy-start.2 = (bf16[128,1536]{1,0:T(8,128)(2,1)S(1)}, bf16[128,1536]{1,0:T(8,128)(2,1)}, u32[]{:S(2)}) copy-start(bf16[128,1536]{1,0:T(8,128)(2,1)} %refs_1_.3) | copy-start | bytes 1179652
  60.0 8.8 %collective-permute-start.16 = (bf16[768,128]{1,0:T(8,128)(2,1)S(1)}, bf16[768,128]{1,0:T(8,128)(2,1)S(1)}, u32[]{:S(2)}, u32[]{:S(2)}) collective-permute-start(bf16[768,128]{1,0:T(8,128)(2,1)S(1)} %shard_map.87), channel_id=1, source_target_pairs={{0,3},{1,2},{2,1},{3,0},{4,7},{5,6},{6,5},{7,4},{8,11},{9,10},{10,... | collective-permute-start | bytes 589832 | tf_op jit(solution)/shard_map/ppermute | solution.py:244
  61.5 9.8 %collective-permute-start.14 = (bf16[768,128]{1,0:T(8,128)(2,1)S(1)}, bf16[768,128]{1,0:T(8,128)(2,1)S(1)}, u32[]{:S(2)}, u32[]{:S(2)}) collective-permute-start(bf16[768,128]{1,0:T(8,128)(2,1)S(1)} %get-tuple-element.23), channel_id=1, source_target_pairs={{0,1},{1,0},{2,3},{3,2},{4,5},{5,4},{6,7},{7,6},{8,9},{9,8},{10,11... | collective-permute-start | bytes 589832 | tf_op jit(solution)/shard_map/ppermute | solution.py:244
  62.1 10.1 %collective-permute-start.15 = (bf16[768,128]{1,0:T(8,128)(2,1)S(1)}, bf16[768,128]{1,0:T(8,128)(2,1)S(1)}, u32[]{:S(2)}, u32[]{:S(2)}) collective-permute-start(bf16[768,128]{1,0:T(8,128)(2,1)S(1)} %get-tuple-element.24), channel_id=1, source_target_pairs={{0,2},{1,3},{2,0},{3,1},{4,6},{5,7},{6,4},{7,5},{8,10},{9,11},{10,... | collective-permute-start | bytes 589832 | tf_op jit(solution)/shard_map/ppermute | solution.py:244
  72.3 15.1 %collective-permute-start.19 = (bf16[768,128]{1,0:T(8,128)(2,1)S(1)}, bf16[768,128]{1,0:T(8,128)(2,1)S(1)}, u32[]{:S(2)}, u32[]{:S(2)}) collective-permute-start(bf16[768,128]{1,0:T(8,128)(2,1)S(1)} %multiply_convert_fusion.refs_0_), channel_id=1, source_target_pairs={{0,2},{1,3},{2,0},{3,1},{4,6},{5,7},{6,4},{7,5},{8,10},{9,11},{10,... | collective-permute-start | bytes 589832 | tf_op jit(solution)/shard_map/ppermute | solution.py:244
  73.0 14.4 %collective-permute-start.18 = (bf16[768,128]{1,0:T(8,128)(2,1)S(1)}, bf16[768,128]{1,0:T(8,128)(2,1)S(1)}, u32[]{:S(2)}, u32[]{:S(2)}) collective-permute-start(bf16[768,128]{1,0:T(8,128)(2,1)S(1)} %multiply_convert_fusion.refs_0_), channel_id=1, source_target_pairs={{0,1},{1,0},{2,3},{3,2},{4,5},{5,4},{6,7},{7,6},{8,9},{9,8},{10,11... | collective-permute-start | bytes 589832 | tf_op jit(solution)/shard_map/ppermute | solution.py:244
  74.5 17.1 %collective-permute-start.17 = (bf16[768,128]{1,0:T(8,128)(2,1)S(1)}, bf16[768,128]{1,0:T(8,128)(2,1)S(1)}, u32[]{:S(2)}, u32[]{:S(2)}) collective-permute-start(bf16[768,128]{1,0:T(8,128)(2,1)S(1)} %multiply_convert_fusion.refs_0_), channel_id=1, source_target_pairs={{0,3},{1,2},{2,1},{3,0},{4,7},{5,6},{6,5},{7,4},{8,11},{9,10},{10,... | collective-permute-start | bytes 589832 | tf_op jit(solution)/shard_map/ppermute | solution.py:244
